TPU v7x, 32 devices: a whole 2x2x4 slice. The times are simulated.
32 devices in a mesh: dp: 4 (over z), tx: 2 (over y), ty: 4 (over x, core).
Axes of the slice: x: 2, y: 2, z: 4, core: 2. Of those that a mesh axis runs over, the one named last changes fastest.
Arguments:
- inputs: bfloat16 [8, 1024, 2048], P('dp', 'ty'), may hold values from -6 to 6
- lengths: int32 [8], replicated, may hold values from 1 to 1024, 5120 in all
- prompt_deal: int32 [8], replicated, may hold values from 0 to 7, each once
- block_owner: int32 [4], replicated, may hold values from 0 to 3, each once
- attn_gain: float32 [2048], replicated, may hold values from 0.5 to 1.5
- latent_gain: float32 [512], replicated, may hold values from 0.5 to 1.5
- final_gain: float32 [2048], replicated, may hold values from 0.5 to 1.5
- w_query: float32 [2048, 3072], P('dp', ('tx', 'ty')), may hold values from -4 to 4
- w_down_kv: float32 [2048, 576], P('dp'), may hold values from -0.125 to 0.125
- w_up_kv: float32 [512, 4096], P('dp', ('tx', 'ty')), may hold values from -4 to 4
- w_out: float32 [2048, 2048], P('dp', 'tx'), may hold values from -0.125 to 0.125
- w_vocab: float32 [2048, 57344], P('dp', ('tx', 'ty')), may hold values from -0.125 to 0.125
Outputs:
- hidden_out: bfloat16 [8, 1024, 2048], P('dp', 'ty', 'tx')
- logits: float32 [8, 57344], P('dp', ('tx', 'ty'))
Inputs may be any that keep to these rules, and one draw needn't show every extreme that they name: `prompt_deal`: a permutation of the 8 prompts. `block_owner`: a permutation of the 4 row blocks. `lengths`: some prompt has exactly 1024 live tokens.
All inputs are finite; a program needn't handle non-finite values.
Results may differ from a plain program's by a relative error of at most 0.0065.
The roundings to bfloat16 on the way count: a program that leaves them out, or rounds other values in their place, can miss the bound.
Values may be sent and summed in bfloat16 or wider, within the bound.
A program may use at most 192 MiB of HBM per device.

v0:
```python
import jax
import jax.numpy as jnp
from jax import lax
from jax.sharding import PartitionSpec as P

NOPE = 128
ROPE = 64
LATENT = 512
LEN = 1024
EPS = 1e-06


def normalize(values, gain):
    wide = values.astype(jnp.float32)
    return wide * lax.rsqrt(jnp.mean(wide * wide, axis=-1, keepdims=True) + EPS) * gain


def rotate(values, position):
    half_dim = values.shape[-1] // 2
    frequency = 10000.0 ** (-jnp.arange(half_dim, dtype=jnp.float32) / half_dim)
    angles = position.astype(jnp.float32)[..., None] * frequency
    cosine = jnp.cos(angles)
    sine = jnp.sin(angles)
    first_half = values[..., :half_dim]
    second_half = values[..., half_dim:]
    return jnp.concatenate(
        [first_half * cosine - second_half * sine, first_half * sine + second_half * cosine],
        axis=-1,
    )


def shards(
    inputs,
    lengths,
    prompt_deal,
    block_owner,
    attn_gain,
    latent_gain,
    final_gain,
    w_query,
    w_down_kv,
    w_up_kv,
    w_out,
    w_vocab,
):
    groups = lax.axis_size("dp")
    inverse = (
        jnp.zeros((groups,), jnp.int32).at[block_owner].set(jnp.arange(groups, dtype=jnp.int32))
    )

    def arrange(gathered):
        block_rows = gathered.shape[0] // groups
        blocks = gathered.reshape((groups, block_rows) + gathered.shape[1:])
        return jnp.take(blocks, inverse, axis=0).reshape(gathered.shape)

    query_w, down_w, up_w, out_w = (
        lax.all_gather(w_query.astype(jnp.bfloat16), "dp", axis=0, tiled=True),
        lax.all_gather(w_down_kv.astype(jnp.bfloat16), "dp", axis=0, tiled=True),
        lax.all_gather(w_up_kv.astype(jnp.bfloat16), "dp", axis=0, tiled=True),
        lax.all_gather(w_out.astype(jnp.bfloat16), "dp", axis=0, tiled=True),
    )
    query_w = arrange(query_w)
    down_w = arrange(down_w)
    up_w = arrange(up_w)
    out_w = arrange(out_w)
    query_w, up_w = (
        lax.all_gather(query_w, "ty", axis=1, tiled=True),
        lax.all_gather(up_w, "ty", axis=1, tiled=True),
    )
    per_grp, quarter, width = inputs.shape
    heads = query_w.shape[1] // (NOPE + ROPE)
    position = lax.axis_index("ty") * quarter + jnp.arange(quarter, dtype=jnp.int32)
    slots = lax.axis_index("dp") * per_grp + jnp.arange(per_grp, dtype=jnp.int32)
    live_len = jnp.take(lengths, jnp.take(prompt_deal, slots))
    flat_rows = inputs.reshape(per_grp * quarter, width)
    normed = normalize(flat_rows, attn_gain).astype(jnp.bfloat16)
    queries = jnp.dot(normed, query_w, preferred_element_type=jnp.float32).reshape(
        per_grp, quarter, heads, NOPE + ROPE
    )
    queries = jnp.concatenate(
        [queries[..., :NOPE], rotate(queries[..., NOPE:], position[None, :, None])], axis=-1
    ).astype(jnp.bfloat16)
    down_proj = jnp.dot(normed, down_w, preferred_element_type=jnp.float32).reshape(
        per_grp, quarter, LATENT + ROPE
    )
    latent = normalize(down_proj[..., :LATENT], latent_gain).astype(jnp.bfloat16)
    key_rope = rotate(down_proj[..., LATENT:], position[None, :]).astype(jnp.bfloat16)
    gathered = lax.all_gather(
        jnp.concatenate([latent, key_rope], axis=-1), "ty", axis=1, tiled=True
    )
    key_val = jnp.dot(gathered[..., :LATENT], up_w, preferred_element_type=jnp.float32).astype(
        jnp.bfloat16
    )
    rope_all = gathered[..., LATENT:]
    key_val = key_val.reshape(per_grp, LEN, heads, 2, NOPE)
    key_nope = key_val[:, :, :, 0]
    values = key_val[:, :, :, 1]
    score_scale = (NOPE + ROPE) ** (-0.5)
    scores = (
        jnp.einsum(
            "pqhd,pkhd->phqk", queries[..., :NOPE], key_nope, preferred_element_type=jnp.float32
        )
        + jnp.einsum(
            "pqhd,pkd->phqk", queries[..., NOPE:], rope_all, preferred_element_type=jnp.float32
        )
    ) * score_scale
    key_pos = jnp.arange(LEN, dtype=jnp.int32)
    allowed = (key_pos[None, None, :] <= position[None, :, None]) & (
        key_pos[None, None, :] < live_len[:, None, None]
    )
    scores = jnp.where(allowed[:, None], scores, -1e30)
    top = jnp.max(scores, axis=-1, keepdims=True)
    expo = jnp.exp(scores - top)
    softmax_w = (expo / jnp.sum(expo, axis=-1, keepdims=True)).astype(jnp.bfloat16)
    attended = jnp.einsum(
        "phqk,pkhd->pqhd", softmax_w, values, preferred_element_type=jnp.float32
    ).astype(jnp.bfloat16)
    attended = attended.reshape(per_grp * quarter, heads * NOPE)
    own_width = width // lax.axis_size("tx")
    col_start = lax.axis_index("tx") * own_width
    partial_value = lax.dot_general(
        attended, out_w, (((1,), (1,)), ((), ())), preferred_element_type=jnp.float32
    ).reshape(per_grp, quarter, width)
    summed = lax.psum_scatter(partial_value, "tx", scatter_dimension=2, tiled=True)
    residual = lax.dynamic_slice_in_dim(inputs, col_start, own_width, 2)
    layer_out = (residual.astype(jnp.float32) + summed).astype(jnp.bfloat16)
    selector = (position[None, :] == (live_len - 1)[:, None]).astype(jnp.float32)
    picked = jnp.einsum("pq,pqd->pd", selector, layer_out.astype(jnp.float32))
    placed = lax.dynamic_update_slice_in_dim(
        jnp.zeros((per_grp, width), jnp.float32), picked, col_start, 1
    )
    last_rows = lax.psum(placed, ("tx", "ty"))
    final_rows = normalize(last_rows, final_gain).astype(jnp.bfloat16)
    vocab_block = arrange(lax.all_gather(w_vocab.astype(jnp.bfloat16), "dp", axis=0, tiled=True))
    logits = jnp.dot(final_rows, vocab_block, preferred_element_type=jnp.float32)
    return (layer_out, logits)


def solution(mesh):
    placed = (
        P("dp", "ty", None),
        P(),
        P(),
        P(),
        P(),
        P(),
        P(),
        P("dp", ("tx", "ty")),
        P("dp", None),
        P("dp", ("tx", "ty")),
        P("dp", "tx"),
        P("dp", ("tx", "ty")),
    )
    return jax.shard_map(
        shards,
        mesh=mesh,
        in_specs=placed,
        out_specs=(P("dp", "ty", "tx"), P("dp", ("tx", "ty"))),
        check_vma=False,
    )
```

profile of v0, /device:TPU:0, one launch (start us, length us, event | category | flops | bytes accessed | tf_op | source)
XLA Modules:
  0.0 1004.1 jit_solution(8479508930206960993)
XLA Ops:
  7.2 2.2 convert_element_type.73
  9.6 1.9 convert_element_type.78
  11.6 2.9 convert_element_type.82
  14.6 0.6 scatter_custom_fusion
  15.2 24.1 %all_gather.26 = bf16[512,512]{1,0:T(8,128)(2,1)S(1)} all-gather(bf16[128,512]{1,0:T(8,128)(2,1)S(1)} %convert_element_type.76), channel_id=1, replica_groups=mesh['dp'=4,'tx'=2,'ty'=4] {'dp'}, dimensions={0}, use_global_device_ids=true | all-gather | bytes 655360 | tf_op jit(solution)/shard_map/all_gather | solution.py:59
  39.3 0.6 gather_fusion.1
  39.9 1.0 bitcast_select_fusion.1
  41.1 0.5 fusion.4
  41.8 27.0 %all-gather.8.cloned.1.call-done = bf16[2048,576]{0,1:T(8,128)(2,1)} async-done(((bf16[512,576]{0,1:T(8,128)(2,1)}), bf16[2048,576]{0,1:T(8,128)(2,1)}) %all-gather.8.cloned.1.call-update) | async-done | bytes 2359312 | tf_op jit(solution)/shard_map/all_gather | solution.py:58
  68.8 1.9 copy.68
  70.7 2.2 gather_fusion
  72.9 2.1 copy.58
  75.2 1.5 fusion.8
  77.0 0.9 pad_maximum_fusion.1
  77.9 29.3 %all-gather.14.cloned.1.call-done = bf16[2048,384]{1,0:T(8,128)(2,1)} async-done(((bf16[512,384]{1,0:T(8,128)(2,1)}), bf16[2048,384]{1,0:T(8,128)(2,1)}) %all-gather.14.cloned.1.call-update) | async-done | bytes 1572880 | tf_op jit(solution)/shard_map/all_gather | solution.py:57
  107.3 2.3 gather_fusion.2
  109.6 0.8 copy.54
  110.4 1.3 broadcast_select_fusion.1
  111.8 0.6 gather_fusion.8
  112.5 0.6 gather_fusion.9
  113.7 75.4 %all-gather.18.cloned.1.call-done = bf16[2048,1024]{1,0:T(8,128)(2,1)} async-done(((bf16[512,1024]{1,0:T(8,128)(2,1)}), bf16[2048,1024]{1,0:T(8,128)(2,1)}) %all-gather.18.cloned.1.call-update) | async-done | bytes 4194320 | tf_op jit(solution)/shard_map/all_gather | solution.py:60
  189.1 4.9 gather_fusion.3
  194.0 4.9 broadcast_select_fusion
  198.9 12.8 %all-gather.12.cloned.1.call-done = bf16[512,2048]{1,0:T(8,128)(2,1)} async-done(((bf16[512,512]{1,0:T(8,128)(2,1)}), bf16[512,2048]{1,0:T(8,128)(2,1)}) %all-gather.12.cloned.1.call-update) | async-done | bytes 2097168 | tf_op jit(solution)/shard_map/all_gather | solution.py:68
  211.7 25.8 %all-gather.10.cloned.1.call-done = bf16[2,1024,576]{1,2,0:T(8,128)(2,1)} async-done(((bf16[2,256,576]{1,2,0:T(8,128)(2,1)}), bf16[2,1024,576]{1,2,0:T(8,128)(2,1)}) %all-gather.10.cloned.1.call-update) | async-done | bytes 2359312 | tf_op jit(solution)/shard_map/all_gather | solution.py:88
  237.5 10.7 %convolution_convert_fusion = bf16[2,1024,2048]{2,1,0:T(8,128)(2,1)} fusion(bf16[2,1024,576]{1,2,0:T(8,128)(2,1)} %all-gather.10.cloned.1.call-done, bf16[512,2048]{1,0:T(8,128)(2,1)} %all-gather.12.cloned.1.call-done), kind=kOutput, calls=%fused_computation.20 | convolution fusion | flops 4299161600 | bytes 12582912 | tf_op jit(solution)/shard_map/dot_general | solution.py:91
  248.1 14.5 %reshape.344 = bf16[2,1024,8,2,128]{4,3,2,1,0:T(2,128)(2,1)} reshape(bf16[2,1024,2048]{2,1,0:T(8,128)(2,1)} %convolution_convert_fusion) | data formatting | bytes 16777216 | tf_op jit(solution)/shard_map/reshape | solution.py:95
  262.6 17.5 %fusion.36 = (bf16[2,1024,8,1,128]{4,3,2,1,0:T(2,128)(2,1)}, bf16[2,1024,8,1,128]{4,3,2,1,0:T(2,128)(2,1)}) fusion(bf16[2,1024,8,2,128]{4,3,2,1,0:T(2,128)(2,1)} %reshape.344), kind=kLoop, calls=%fused_computation.93 | loop fusion | bytes 16777216 | tf_op jit(solution)/shard_map/slice | solution.py:97
  280.1 20.1 %copy.55 = bf16[2,1024,8,1,128]{1,4,2,0,3:T(8,128)(2,1)} copy(bf16[2,1024,8,1,128]{4,3,2,1,0:T(2,128)(2,1)} %get-tuple-element.9) | data formatting | bytes 8388608
  300.2 5.7 fusion.13
  306.0 1.6 copy-done.8
  307.8 9.1 fusion.22
  316.8 17.3 %fusion.37 = (f32[2,8,256]{2,1,0:T(8,128)S(1)}, f32[2,8,256,1024]{3,2,1,0:T(8,128)}) fusion(f32[2,1024,256,8]{1,2,3,0:T(8,128)} %fusion.22, pred[2,256,1024]{2,1,0:T(8,128)(4,1)S(1)} %broadcast_and_fusion, bf16[2,1024,8,1,128]{4,3,2,1,0:T(2,128)(2,1)} %get-tuple-element.10, f32[2,256,8,192]{1,3,2,0:T(8,128)} %copy-done.8), kind=kOutput, calls=%fused_computation.94 | convolution fusion | flops 1094714368 | bytes 43532288 | tf_op jit(solution)/shard_map/sub | solution.py:113
  334.1 8.8 fusion.18
  342.9 4.4 fusion.38
  347.4 9.2 convert_element_type.85
  356.7 45.0 %reduce-scatter.2.cloned.1.call-done = f32[2,256,1024]{2,1,0:T(8,128)} async-done(((f32[2,256,2048]{2,1,0:T(8,128)}), f32[2,256,1024]{2,1,0:T(8,128)}) %reduce-scatter.2.cloned.1.call-update) | async-done | bytes 2097168 | tf_op jit(solution)/shard_map/reduce_scatter | solution.py:124
  401.7 2.0 add_convert_fusion
  404.0 23.1 %psum.7 = f32[2,2048]{1,0:T(2,128)S(1)} all-reduce(f32[2,2048]{1,0:T(2,128)S(1)} %bitcast_dynamic-update-slice_fusion), channel_id=1, replica_groups=mesh['dp'=4,'tx'=2,'ty'=4] {'tx','ty'}, use_global_device_ids=true, to_apply=%region_6.8 | all-reduce | flops 4096 | bytes 32768 | tf_op jit(solution)/shard_map/psum | solution.py:132
  427.2 469.4 %all-gather.20.cloned.1.call-done = bf16[2048,7168]{1,0:T(8,128)(2,1)} async-done(((bf16[512,7168]{1,0:T(8,128)(2,1)}), bf16[2048,7168]{1,0:T(8,128)(2,1)}) %all-gather.20.cloned.1.call-update) | async-done | bytes 29360144 | tf_op jit(solution)/shard_map/all_gather | solution.py:134
  896.5 20.0 %fusion.35 = (bf16[4,512,1792]{2,1,0:T(8,128)(2,1)}, bf16[4,512,1792]{2,1,0:T(8,128)(2,1)}, bf16[4,512,1792]{2,1,0:T(8,128)(2,1)}, bf16[4,512,1792]{2,1,0:T(8,128)(2,1)}) fusion(bf16[4,512,7168]{2,1,0:T(8,128)(2,1)} %bitcast.74), kind=kLoop, calls=%fused_computation.92 | loop fusion | bytes 58720256 | tf_op jit(solution)/shard_map/jit(_take)/gather | solution.py:54
  916.6 7.1 gather_fusion.7
  923.7 7.0 gather_fusion.6
  930.7 7.0 gather_fusion.5
  937.8 7.1 gather_fusion.4
  944.9 20.2 %pad_maximum_fusion = bf16[4,512,7168]{2,1,0:T(8,128)(2,1)} fusion(bf16[4,512,1792]{2,1,0:T(8,128)(2,1)} %gather_fusion.7, bf16[4,512,1792]{2,1,0:T(8,128)(2,1)} %gather_fusion.6, bf16[4,512,1792]{2,1,0:T(8,128)(2,1)} %gather_fusion.5, bf16[4,512,1792]{2,1,0:T(8,128)(2,1)} %gather_fusion.4), kind=kLoop, calls=%fused_computation.12 | loop fusion | flops 117440512 | bytes 58720256
  965.1 20.2 %bitcast_select_fusion = bf16[2048,7168]{1,0:T(8,128)(2,1)} fusion(bf16[4,512,7168]{2,1,0:T(8,128)(2,1)} %pad_maximum_fusion, pred[2048]{0:T(1024)(128)(4,1)S(1)} %bitcast.86), kind=kLoop, calls=%fused_computation.13 | loop fusion | flops 14680064 | bytes 58722304 | tf_op jit(solution)/shard_map/jit(_take)/select_n | solution.py:54
  985.3 12.0 %fusion.26 = f32[2,7168]{1,0:T(2,128)} fusion(bf16[2048,7168]{1,0:T(8,128)(2,1)} %bitcast_select_fusion, f32[2,2048]{1,0:T(2,128)S(1)} %psum.7, f32[2]{0:T(128)S(1)} %add_rsqrt_fusion.2, f32[2048]{0:T(1024)S(1)} %copy-done.10), kind=kOutput, calls=%fused_computation.62 | convolution fusion | flops 58732544 | bytes 29442056 | tf_op jit(solution)/shard_map/dot_general | solution.py:135
  (76 shorter events, 2.7 us)
Async XLA Ops:
  7.2 104.6 %copy-start = (s32[8]{0:T(128)S(1)}, s32[8]{0:T(128)}, u32[]{:S(2)}) copy-start(s32[8]{0:T(128)} %param.16) | copy-start | bytes 100
  7.2 7.3 copy-start.9
  7.2 7.3 copy-start.13
  7.2 61.6 %all-gather.8.cloned.1.call-start = ((), (), s32[]{:S(2)}) async-start(), calls=%async_computation.1 | async-start | bytes 2949120 | tf_op jit(solution)/shard_map/all_gather | solution.py:58
  9.5 97.8 %all-gather.14.cloned.1.call-start = ((), (), s32[]{:S(2)}) async-start(), calls=%async_computation.4 | async-start | bytes 1966080 | tf_op jit(solution)/shard_map/all_gather | solution.py:57
  11.5 29.6 %copy-start.3 = (bf16[2,256,2048]{2,1,0:T(8,128)(2,1)S(1)}, bf16[2,256,2048]{2,1,0:T(8,128)(2,1)}, u32[]{:S(2)}) copy-start(bf16[2,256,2048]{2,1,0:T(8,128)(2,1)} %param.14) | copy-start | bytes 6291460
  11.5 177.6 %all-gather.18.cloned.1.call-start = ((), (), s32[]{:S(2)}) async-start(), calls=%async_computation.6 | async-start | bytes 5242880 | tf_op jit(solution)/shard_map/all_gather | solution.py:60
  14.4 197.2 %all-gather.12.cloned.1.call-start = ((), (), s32[]{:S(2)}) async-start(), calls=%async_computation.3 | async-start | bytes 2621440 | tf_op jit(solution)/shard_map/all_gather | solution.py:68
  40.9 196.5 %all-gather.10.cloned.1.call-start = ((), (), s32[]{:S(2)}) async-start(), calls=%async_computation.2 | async-start | bytes 2949120 | tf_op jit(solution)/shard_map/all_gather | solution.py:88
  70.7 4.3 copy-start.12
  72.9 2.3 copy-start.4
  75.2 1.7 copy-start.11
  77.9 222.3 %all-gather.16.cloned.1.call-start = ((), (), s32[]{:S(2)}) async-start(), calls=%async_computation.5 | async-start | bytes 7864320 | tf_op jit(solution)/shard_map/all_gather | solution.py:67
  109.6 2.9 copy-start.2
  111.7 290.0 %reduce-scatter.2.cloned.1.call-start = ((), (), s32[]{:S(2)}) async-start(), calls=%async_computation.7 | async-start | bytes 6291456 | tf_op jit(solution)/shard_map/reduce_scatter | solution.py:124
  280.1 20.1 %copy-start.5 = (bf16[2,256,2048]{2,1,0:T(8,128)(2,1)S(1)}, bf16[2,256,2048]{2,1,0:T(8,128)(2,1)}, u32[]{:S(2)}) copy-start(bf16[2,256,2048]{2,1,0:T(8,128)(2,1)} %param.14) | copy-start | bytes 6291460
  305.9 1.6 copy-start.8
  334.1 8.8 copy-start.7
  347.3 549.2 %all-gather.20.cloned.1.call-start = ((), (), s32[]{:S(2)}) async-start(), calls=%async_computation.8 | async-start | bytes 36700160 | tf_op jit(solution)/shard_map/all_gather | solution.py:134
  403.7 512.9 %copy-start.6 = (bf16[2,256,1024]{2,1,0:T(8,128)(2,1)}, bf16[2,256,1024]{2,1,0:T(8,128)(2,1)S(1)}, u32[]{:S(2)}) copy-start(bf16[2,256,1024]{2,1,0:T(8,128)(2,1)S(1)} %add_convert_fusion) | copy-start | bytes 3145732
  965.1 20.2 %copy-start.10 = (f32[2048]{0:T(1024)S(1)}, f32[2048]{0:T(1024)}, u32[]{:S(2)}) copy-start(f32[2048]{0:T(1024)} %param.20) | copy-start | bytes 24580
  985.2 12.0 %copy-start.1 = (s32[8]{0:T(128)S(1)}, s32[8]{0:T(128)}, u32[]{:S(2)}) copy-start(s32[8]{0:T(128)} %param.16) | copy-start | bytes 100
Sparse Core Ops, SparseCore 0:
  9.6 59.1 all-gather.7
  70.4 36.8 all-gather.13
  109.4 79.6 all-gather.17
  190.5 21.1 all-gather.11
  213.1 24.3 all-gather.9
  238.9 46.3 all-gather.15
  347.4 54.2 reduce-scatter.1
  403.4 493.1 all-gather.19
where the time goes:
time: 1010 us; the launch traced here: 1000 us
  waiting for transfers between devices  685 us (68%)
  local copies, waits for them, and re-layouts  119 us (12%)
  matrix products  69.7 us (7%)
  other arithmetic  68.5 us (7%)
  blocking collectives  47.2 us (5%)
  between operations  14.5 us (1%)
    all_gather x1, waiting for transfers between devices, shards(): lax.all_gather(w_vocab.astype(jnp.bfloat16), 'dp', axis=0, tiled=True)  469 us
    all_gather x1, waiting for transfers between devices, shards(): lax.all_gather(w_out.astype(jnp.bfloat16), 'dp', axis=0, tiled=True)  75.4 us
    gather x11, local copies, waits for them, and re-layouts, arrange(): return jnp.take(blocks, inverse, axis=0).reshape(gathered.shape)  61.2 us
    reduce_scatter x1, waiting for transfers between devices, shards(): lax.psum_scatter(partial_value, 'tx', scatter_dimension=2, tiled=True)  45 us
    all_gather x1, waiting for transfers between devices, shards(): lax.all_gather(w_query.astype(jnp.bfloat16), 'dp', axis=0, tiled=True)  29.3 us
    select_n x5, other arithmetic, arrange(): return jnp.take(blocks, inverse, axis=0).reshape(gathered.shape)  27.3 us
    all_gather x1, waiting for transfers between devices, shards(): lax.all_gather(w_down_kv.astype(jnp.bfloat16), 'dp', axis=0, tiled=True)  27 us
    all_gather x1, waiting for transfers between devices, shards(): lax.all_gather(jnp.concatenate([latent, key_rope], axis=-1), 'ty', axis=1...  25.8 us
  transfers between devices with their start and end apart: 8, of which 7 were waited for; matrix products, arithmetic and copies ran while one was open for 11% of the time, Pallas kernels for 0%

commit v1 on v0

--- a/solution.py
+++ b/solution.py
@@ -129,7 +129,8 @@
     placed = lax.dynamic_update_slice_in_dim(
         jnp.zeros((per_grp, width), jnp.float32), picked, col_start, 1
     )
-    last_rows = lax.psum(placed, ("tx", "ty"))
+    inner = lax.psum(placed, "ty")
+    last_rows = lax.psum(inner, "tx")
     final_rows = normalize(last_rows, final_gain).astype(jnp.bfloat16)
     vocab_block = arrange(lax.all_gather(w_vocab.astype(jnp.bfloat16), "dp", axis=0, tiled=True))
     logits = jnp.dot(final_rows, vocab_block, preferred_element_type=jnp.float32)

time: 1010 us -> 1010 us (level)
    psum x1 -> x2, blocking collectives: 23.1 us -> 18.4 us  [the longest x1 11.2 us: shards(): inner = lax.psum(placed, 'ty')]
where the time goes in v1:
time: 1010 us; the launch traced here: 1000 us
  waiting for transfers between devices  689 us (68%)
  local copies, waits for them, and re-layouts  119 us (12%)
  matrix products  69.7 us (7%)
  other arithmetic  68.7 us (7%)
  blocking collectives  42.5 us (4%)
  between operations  14.5 us (1%)
    all_gather x1, waiting for transfers between devices, shards(): lax.all_gather(w_vocab.astype(jnp.bfloat16), 'dp', axis=0, tiled=True)  474 us
    all_gather x1, waiting for transfers between devices, shards(): lax.all_gather(w_out.astype(jnp.bfloat16), 'dp', axis=0, tiled=True)  75.4 us
    gather x11, local copies, waits for them, and re-layouts, arrange(): return jnp.take(blocks, inverse, axis=0).reshape(gathered.shape)  61.2 us
    reduce_scatter x1, waiting for transfers between devices, shards(): lax.psum_scatter(partial_value, 'tx', scatter_dimension=2, tiled=True)  45 us
    all_gather x1, waiting for transfers between devices, shards(): lax.all_gather(w_query.astype(jnp.bfloat16), 'dp', axis=0, tiled=True)  29.3 us
    select_n x5, other arithmetic, arrange(): return jnp.take(blocks, inverse, axis=0).reshape(gathered.shape)  27.4 us
    all_gather x1, waiting for transfers between devices, shards(): lax.all_gather(w_down_kv.astype(jnp.bfloat16), 'dp', axis=0, tiled=True)  27 us
    all_gather x1, waiting for transfers between devices, shards(): lax.all_gather(jnp.concatenate([latent, key_rope], axis=-1), 'ty', axis=1...  25.8 us
  transfers between devices with their start and end apart: 8, of which 7 were waited for; matrix products, arithmetic and copies ran while one was open for 11% of the time, Pallas kernels for 0%

profile of v1, /device:TPU:0, one launch (start us, length us, event | category | flops | bytes accessed | tf_op | source)
XLA Modules:
  0.0 1004.2 jit_solution(5274765796002045988)
XLA Ops:
  7.2 2.2 convert_element_type.73
  9.6 1.9 convert_element_type.78
  11.6 2.9 convert_element_type.82
  14.6 0.6 scatter_custom_fusion
  15.2 24.1 %all_gather.26 = bf16[512,512]{1,0:T(8,128)(2,1)S(1)} all-gather(bf16[128,512]{1,0:T(8,128)(2,1)S(1)} %convert_element_type.76), channel_id=1, replica_groups=mesh['dp'=4,'tx'=2,'ty'=4] {'dp'}, dimensions={0}, use_global_device_ids=true | all-gather | bytes 655360 | tf_op jit(solution)/shard_map/all_gather | solution.py:59
  39.3 0.6 gather_fusion.1
  40.0 1.0 bitcast_select_fusion.1
  41.8 27.0 %all-gather.8.cloned.1.call-done = bf16[2048,576]{0,1:T(8,128)(2,1)} async-done(((bf16[512,576]{0,1:T(8,128)(2,1)}), bf16[2048,576]{0,1:T(8,128)(2,1)}) %all-gather.8.cloned.1.call-update) | async-done | bytes 2359312 | tf_op jit(solution)/shard_map/all_gather | solution.py:58
  68.8 1.9 copy.68
  70.7 2.2 gather_fusion
  72.9 2.1 copy.58
  75.2 1.5 fusion.8
  77.0 0.9 pad_maximum_fusion.1
  78.0 29.3 %all-gather.14.cloned.1.call-done = bf16[2048,384]{1,0:T(8,128)(2,1)} async-done(((bf16[512,384]{1,0:T(8,128)(2,1)}), bf16[2048,384]{1,0:T(8,128)(2,1)}) %all-gather.14.cloned.1.call-update) | async-done | bytes 1572880 | tf_op jit(solution)/shard_map/all_gather | solution.py:57
  107.3 2.3 gather_fusion.2
  109.6 0.8 copy.54
  110.4 1.3 broadcast_select_fusion.1
  111.8 0.6 gather_fusion.8
  112.5 0.6 gather_fusion.9
  113.7 75.4 %all-gather.18.cloned.1.call-done = bf16[2048,1024]{1,0:T(8,128)(2,1)} async-done(((bf16[512,1024]{1,0:T(8,128)(2,1)}), bf16[2048,1024]{1,0:T(8,128)(2,1)}) %all-gather.18.cloned.1.call-update) | async-done | bytes 4194320 | tf_op jit(solution)/shard_map/all_gather | solution.py:60
  189.1 4.9 gather_fusion.3
  194.1 4.9 broadcast_select_fusion
  198.9 12.8 %all-gather.12.cloned.1.call-done = bf16[512,2048]{1,0:T(8,128)(2,1)} async-done(((bf16[512,512]{1,0:T(8,128)(2,1)}), bf16[512,2048]{1,0:T(8,128)(2,1)}) %all-gather.12.cloned.1.call-update) | async-done | bytes 2097168 | tf_op jit(solution)/shard_map/all_gather | solution.py:68
  211.7 25.8 %all-gather.10.cloned.1.call-done = bf16[2,1024,576]{1,2,0:T(8,128)(2,1)} async-done(((bf16[2,256,576]{1,2,0:T(8,128)(2,1)}), bf16[2,1024,576]{1,2,0:T(8,128)(2,1)}) %all-gather.10.cloned.1.call-update) | async-done | bytes 2359312 | tf_op jit(solution)/shard_map/all_gather | solution.py:88
  237.5 10.7 %convolution_convert_fusion = bf16[2,1024,2048]{2,1,0:T(8,128)(2,1)} fusion(bf16[2,1024,576]{1,2,0:T(8,128)(2,1)} %all-gather.10.cloned.1.call-done, bf16[512,2048]{1,0:T(8,128)(2,1)} %all-gather.12.cloned.1.call-done), kind=kOutput, calls=%fused_computation.20 | convolution fusion | flops 4299161600 | bytes 12582912 | tf_op jit(solution)/shard_map/dot_general | solution.py:91
  248.2 14.5 %reshape.344 = bf16[2,1024,8,2,128]{4,3,2,1,0:T(2,128)(2,1)} reshape(bf16[2,1024,2048]{2,1,0:T(8,128)(2,1)} %convolution_convert_fusion) | data formatting | bytes 16777216 | tf_op jit(solution)/shard_map/reshape | solution.py:95
  262.6 17.5 %fusion.36 = (bf16[2,1024,8,1,128]{4,3,2,1,0:T(2,128)(2,1)}, bf16[2,1024,8,1,128]{4,3,2,1,0:T(2,128)(2,1)}) fusion(bf16[2,1024,8,2,128]{4,3,2,1,0:T(2,128)(2,1)} %reshape.344), kind=kLoop, calls=%fused_computation.93 | loop fusion | bytes 16777216 | tf_op jit(solution)/shard_map/slice | solution.py:97
  280.1 20.2 %copy.55 = bf16[2,1024,8,1,128]{1,4,2,0,3:T(8,128)(2,1)} copy(bf16[2,1024,8,1,128]{4,3,2,1,0:T(2,128)(2,1)} %get-tuple-element.9) | data formatting | bytes 8388608
  300.3 5.7 fusion.13
  306.0 1.6 copy-done.8
  307.8 9.1 fusion.22
  316.9 17.3 %fusion.37 = (f32[2,8,256]{2,1,0:T(8,128)S(1)}, f32[2,8,256,1024]{3,2,1,0:T(8,128)}) fusion(f32[2,1024,256,8]{1,2,3,0:T(8,128)} %fusion.22, pred[2,256,1024]{2,1,0:T(8,128)(4,1)S(1)} %broadcast_and_fusion, bf16[2,1024,8,1,128]{4,3,2,1,0:T(2,128)(2,1)} %get-tuple-element.10, f32[2,256,8,192]{1,3,2,0:T(8,128)} %copy-done.8), kind=kOutput, calls=%fused_computation.94 | convolution fusion | flops 1094714368 | bytes 43532288 | tf_op jit(solution)/shard_map/sub | solution.py:113
  334.2 8.8 fusion.18
  343.0 4.4 fusion.38
  347.4 9.2 convert_element_type.85
  356.7 45.0 %reduce-scatter.2.cloned.1.call-done = f32[2,256,1024]{2,1,0:T(8,128)} async-done(((f32[2,256,2048]{2,1,0:T(8,128)}), f32[2,256,1024]{2,1,0:T(8,128)}) %reduce-scatter.2.cloned.1.call-update) | async-done | bytes 2097168 | tf_op jit(solution)/shard_map/reduce_scatter | solution.py:124
  401.7 2.0 add_convert_fusion
  404.0 11.2 %psum.14 = f32[2,2048]{1,0:T(2,128)S(1)} all-reduce(f32[2,2048]{1,0:T(2,128)S(1)} %bitcast_dynamic-update-slice_fusion), channel_id=1, replica_groups=mesh['dp'=4,'tx'=2,'ty'=4] {'ty'}, use_global_device_ids=true, to_apply=%region_6.8 | all-reduce | flops 4096 | bytes 32768 | tf_op jit(solution)/shard_map/psum | solution.py:132
  415.1 7.2 psum.15
  422.5 474.0 %all-gather.20.cloned.1.call-done = bf16[2048,7168]{1,0:T(8,128)(2,1)} async-done(((bf16[512,7168]{1,0:T(8,128)(2,1)}), bf16[2048,7168]{1,0:T(8,128)(2,1)}) %all-gather.20.cloned.1.call-update) | async-done | bytes 29360144 | tf_op jit(solution)/shard_map/all_gather | solution.py:135
  896.5 20.0 %fusion.35 = (bf16[4,512,1792]{2,1,0:T(8,128)(2,1)}, bf16[4,512,1792]{2,1,0:T(8,128)(2,1)}, bf16[4,512,1792]{2,1,0:T(8,128)(2,1)}, bf16[4,512,1792]{2,1,0:T(8,128)(2,1)}) fusion(bf16[4,512,7168]{2,1,0:T(8,128)(2,1)} %bitcast.74), kind=kLoop, calls=%fused_computation.92 | loop fusion | bytes 58720256 | tf_op jit(solution)/shard_map/jit(_take)/gather | solution.py:54
  916.6 7.1 gather_fusion.7
  923.7 7.0 gather_fusion.6
  930.7 7.1 gather_fusion.5
  937.8 7.1 gather_fusion.4
  944.9 20.2 %pad_maximum_fusion = bf16[4,512,7168]{2,1,0:T(8,128)(2,1)} fusion(bf16[4,512,1792]{2,1,0:T(8,128)(2,1)} %gather_fusion.7, bf16[4,512,1792]{2,1,0:T(8,128)(2,1)} %gather_fusion.6, bf16[4,512,1792]{2,1,0:T(8,128)(2,1)} %gather_fusion.5, bf16[4,512,1792]{2,1,0:T(8,128)(2,1)} %gather_fusion.4), kind=kLoop, calls=%fused_computation.12 | loop fusion | flops 117440512 | bytes 58720256
  965.1 20.3 %bitcast_select_fusion = bf16[2048,7168]{1,0:T(8,128)(2,1)} fusion(bf16[4,512,7168]{2,1,0:T(8,128)(2,1)} %pad_maximum_fusion, pred[2048]{0:T(1024)(128)(4,1)S(1)} %bitcast.86), kind=kLoop, calls=%fused_computation.13 | loop fusion | flops 14680064 | bytes 58722304 | tf_op jit(solution)/shard_map/jit(_take)/select_n | solution.py:54
  985.4 12.0 %fusion.26 = f32[2,7168]{1,0:T(2,128)} fusion(bf16[2048,7168]{1,0:T(8,128)(2,1)} %bitcast_select_fusion, f32[2,2048]{1,0:T(2,128)S(1)} %psum.15, f32[2]{0:T(128)S(1)} %add_rsqrt_fusion.2, f32[2048]{0:T(1024)S(1)} %copy-done.10), kind=kOutput, calls=%fused_computation.62 | convolution fusion | flops 58732544 | bytes 29442056 | tf_op jit(solution)/shard_map/dot_general | solution.py:136
  (77 shorter events, 3.2 us)
Async XLA Ops:
  7.2 104.6 %copy-start = (s32[8]{0:T(128)S(1)}, s32[8]{0:T(128)}, u32[]{:S(2)}) copy-start(s32[8]{0:T(128)} %param.16) | copy-start | bytes 100
  7.2 7.3 copy-start.9
  7.2 7.4 copy-start.13
  7.2 61.6 %all-gather.8.cloned.1.call-start = ((), (), s32[]{:S(2)}) async-start(), calls=%async_computation.1 | async-start | bytes 2949120 | tf_op jit(solution)/shard_map/all_gather | solution.py:58
  9.5 97.8 %all-gather.14.cloned.1.call-start = ((), (), s32[]{:S(2)}) async-start(), calls=%async_computation.4 | async-start | bytes 1966080 | tf_op jit(solution)/shard_map/all_gather | solution.py:57
  11.5 29.6 %copy-start.3 = (bf16[2,256,2048]{2,1,0:T(8,128)(2,1)S(1)}, bf16[2,256,2048]{2,1,0:T(8,128)(2,1)}, u32[]{:S(2)}) copy-start(bf16[2,256,2048]{2,1,0:T(8,128)(2,1)} %param.14) | copy-start | bytes 6291460
  11.5 177.6 %all-gather.18.cloned.1.call-start = ((), (), s32[]{:S(2)}) async-start(), calls=%async_computation.6 | async-start | bytes 5242880 | tf_op jit(solution)/shard_map/all_gather | solution.py:60
  14.5 197.2 %all-gather.12.cloned.1.call-start = ((), (), s32[]{:S(2)}) async-start(), calls=%async_computation.3 | async-start | bytes 2621440 | tf_op jit(solution)/shard_map/all_gather | solution.py:68
  41.0 196.5 %all-gather.10.cloned.1.call-start = ((), (), s32[]{:S(2)}) async-start(), calls=%async_computation.2 | async-start | bytes 2949120 | tf_op jit(solution)/shard_map/all_gather | solution.py:88
  70.7 4.3 copy-start.12
  72.9 2.3 copy-start.4
  75.2 1.7 copy-start.11
  77.9 222.3 %all-gather.16.cloned.1.call-start = ((), (), s32[]{:S(2)}) async-start(), calls=%async_computation.5 | async-start | bytes 7864320 | tf_op jit(solution)/shard_map/all_gather | solution.py:67
  109.6 2.8 copy-start.2
  111.7 290.0 %reduce-scatter.2.cloned.1.call-start = ((), (), s32[]{:S(2)}) async-start(), calls=%async_computation.7 | async-start | bytes 6291456 | tf_op jit(solution)/shard_map/reduce_scatter | solution.py:124
  280.1 20.2 %copy-start.5 = (bf16[2,256,2048]{2,1,0:T(8,128)(2,1)S(1)}, bf16[2,256,2048]{2,1,0:T(8,128)(2,1)}, u32[]{:S(2)}) copy-start(bf16[2,256,2048]{2,1,0:T(8,128)(2,1)} %param.14) | copy-start | bytes 6291460
  306.0 1.6 copy-start.8
  334.2 8.8 copy-start.7
  347.4 549.2 %all-gather.20.cloned.1.call-start = ((), (), s32[]{:S(2)}) async-start(), calls=%async_computation.8 | async-start | bytes 36700160 | tf_op jit(solution)/shard_map/all_gather | solution.py:135
  403.7 512.9 %copy-start.6 = (bf16[2,256,1024]{2,1,0:T(8,128)(2,1)}, bf16[2,256,1024]{2,1,0:T(8,128)(2,1)S(1)}, u32[]{:S(2)}) copy-start(bf16[2,256,1024]{2,1,0:T(8,128)(2,1)S(1)} %add_convert_fusion) | copy-start | bytes 3145732
  965.0 20.3 %copy-start.10 = (f32[2048]{0:T(1024)S(1)}, f32[2048]{0:T(1024)}, u32[]{:S(2)}) copy-start(f32[2048]{0:T(1024)} %param.20) | copy-start | bytes 24580
  985.4 12.0 %copy-start.1 = (s32[8]{0:T(128)S(1)}, s32[8]{0:T(128)}, u32[]{:S(2)}) copy-start(s32[8]{0:T(128)} %param.16) | copy-start | bytes 100
Sparse Core Ops, SparseCore 0:
  9.6 59.1 all-gather.7
  70.4 36.8 all-gather.13
  109.5 79.6 all-gather.17
  190.5 21.1 all-gather.11
  213.1 24.3 all-gather.9
  238.9 46.3 all-gather.15
  347.5 54.1 reduce-scatter.1
  403.4 493.1 all-gather.19
